TPU v7x, 32 devices: a whole 2x2x4 slice. The times are simulated.
32 devices in a mesh: hst: 4 (over x, core), dev: 8 (over z, y).
Axes of the slice: x: 2, y: 2, z: 4, core: 2. Of those that a mesh axis runs over, the one named last changes fastest.
Arguments:
- features: float32 [524288, 128], P(('hst', 'dev')), may hold values from -6 to 6
- requests: int32 [1024, 256], P(('hst', 'dev')), may hold values from 0 to 16383
- adjacent_one: int32 [135168, 15], P(('hst', 'dev')), may hold values from 0 to 8191, as said below
- adjacent_two: int32 [12288, 10], P(('hst', 'dev')), may hold values from 0 to 4223
- adjacent_three: int32 [2048, 5], P(('hst', 'dev')), may hold values from 0 to 383
- valid_one: int32 [135168, 15], P(('hst', 'dev')), may hold values from 0 to 1, as said below
- valid_two: int32 [12288, 10], P(('hst', 'dev')), may hold values from 0 to 1
- valid_three: int32 [2048, 5], P(('hst', 'dev')), may hold values from 0 to 1
- labels: int32 [2048], P(('hst', 'dev')), may hold values from 0 to 171
- labelled: int32 [2048], P(('hst', 'dev')), may hold values from 0 to 1, as said below
- weights_in: float32 [2, 128, 256], replicated, may hold values from -0.5 to 0.5
- weights_mid: float32 [2, 256, 256], replicated, may hold values from -0.375 to 0.375
- weights_out: float32 [2, 256, 172], replicated, may hold values from -0.375 to 0.375
- biases: float32 [684], replicated, may hold values from -0.6 to 0.6
- moment_one: float32 [684], replicated, may hold values from -0.0007954951 to 0.0007954951
- moment_two: float32 [684], replicated, may hold values from 6.1035155e-07 to 2.4414062e-06
- step_count: int32 [], replicated, may hold values from 2 to 20
- left_in: float32 [2, 128, 128], replicated, as said below
- left_mid: float32 [2, 256, 256], replicated, as said below
- left_out: float32 [2, 256, 256], replicated, as said below
- right_in: float32 [2, 256, 256], replicated, as said below
- right_mid: float32 [2, 256, 256], replicated, as said below
- right_out: float32 [2, 172, 172], replicated, as said below
- invleft_in: float32 [2, 128, 128], replicated, as said below
- invleft_mid: float32 [2, 256, 256], replicated, as said below
- invleft_out: float32 [2, 256, 256], replicated, as said below
- invright_in: float32 [2, 256, 256], replicated, as said below
- invright_mid: float32 [2, 256, 256], replicated, as said below
- invright_out: float32 [2, 172, 172], replicated, as said below
Outputs:
- loss: float32 [], replicated
- new_weights_in: float32 [2, 128, 256], replicated
- new_weights_mid: float32 [2, 256, 256], replicated
- new_weights_out: float32 [2, 256, 172], replicated
- copy_in: bfloat16 [2, 128, 256], replicated
- copy_mid: bfloat16 [2, 256, 256], replicated
- copy_out: bfloat16 [2, 256, 172], replicated
- new_left_in: float32 [2, 128, 128], replicated
- new_left_mid: float32 [2, 256, 256], replicated
- new_left_out: float32 [2, 256, 256], replicated
- new_right_in: float32 [2, 256, 256], replicated
- new_right_mid: float32 [2, 256, 256], replicated
- new_right_out: float32 [2, 172, 172], replicated
- new_biases: float32 [684], replicated
- new_moment_one: float32 [684], replicated
- new_moment_two: float32 [684], replicated
Inputs may be any that keep to these rules, and one draw needn't show every extreme that they name: `adjacent_one`: every one of a device's 8192 pulled slots is named by some entry of its rows. `valid_one`: valid shares differ from device to device. The first seed of every device is labelled. `left_in`: a positive multiple of the identity in each of the two matrices. `left_mid`: a positive multiple of the identity in each of the two matrices. `left_out`: a positive multiple of the identity in each of the two matrices. `right_in`: a positive multiple of the identity in each of the two matrices. `right_mid`: a positive multiple of the identity in each of the two matrices. `right_out`: a positive multiple of the identity in each of the two matrices. `invleft_in`: symmetric. `invleft_mid`: symmetric. `invleft_out`: symmetric. `invright_in`: symmetric. `invright_mid`: symmetric. `invright_out`: symmetric.
All inputs are finite; a program needn't handle non-finite values.
Results may differ from a plain program's by a relative error of at most 0.0094.
Values may be sent and summed in bfloat16 or wider, within the bound.
No kernel may reach another device: no remote copies, remote signals or barrier semaphores. Data moves between devices by JAX's collectives and lax.ppermute only.
A program may use at most 128 MiB of HBM per device.

v0:
```python
import jax
import jax.numpy as jnp
from jax import lax
from jax.sharding import PartitionSpec as P

highest = lax.Precision.HIGHEST


def pull_features(features, requests):
    width = features.shape[1]
    found = features[
        lax.all_to_all(requests, ("hst", "dev"), split_axis=0, concat_axis=0, tiled=True)
    ].astype(jnp.bfloat16)
    arrived = lax.all_to_all(found, ("hst", "dev"), split_axis=0, concat_axis=0, tiled=True)
    return arrived.reshape(-1, width)


def mask_counts(valid_mask):
    weights = valid_mask.astype(jnp.float32)
    return (weights, jnp.maximum(jnp.sum(weights, axis=1), 1.0))


def forward_layer(source, adjacent, valid_mask, weight, bias_row):
    weights, counts = mask_counts(valid_mask)
    summed = jnp.zeros((adjacent.shape[0], source.shape[1]), jnp.float32)
    for column in range(adjacent.shape[1]):
        summed = (
            summed
            + source[adjacent[:, column]].astype(jnp.float32) * weights[:, column : column + 1]
        )
    mixed = (summed / counts[:, None]).astype(jnp.bfloat16)
    selfrows = source[: adjacent.shape[0]]
    preact = (
        jnp.dot(selfrows, weight[0], preferred_element_type=jnp.float32)
        + jnp.dot(mixed, weight[1], preferred_element_type=jnp.float32)
        + bias_row
    )
    return (preact, mixed)


def silu_slope(preact):
    sigma = jax.nn.sigmoid(preact)
    return sigma * (1.0 + preact * (1.0 - sigma))


def contract_rows(left_side, right_side):
    return lax.dot_general(
        left_side, right_side, (((0,), (0,)), ((), ())), preferred_element_type=jnp.float32
    )


def contract_cols(left_side, right_side):
    return lax.dot_general(
        left_side, right_side, (((1,), (1,)), ((), ())), preferred_element_type=jnp.float32
    )


def backward_layer(grad_pre, source, adjacent, valid_mask, mixed, weight, going_down):
    row_count = adjacent.shape[0]
    selfrows = source[:row_count]
    grad_weight = jnp.stack([contract_rows(selfrows, grad_pre), contract_rows(mixed, grad_pre)])
    grad_bias = jnp.sum(grad_pre.astype(jnp.float32), axis=0)
    if not going_down:
        return (grad_weight, grad_bias, None)
    weights, counts = mask_counts(valid_mask)
    to_self = contract_cols(grad_pre, weight[0])
    to_mixed = contract_cols(grad_pre, weight[1]) / counts[:, None]
    grad_source = jnp.zeros(source.shape, jnp.float32).at[:row_count].add(to_self)
    for column in range(adjacent.shape[1]):
        grad_source = grad_source.at[adjacent[:, column]].add(
            to_mixed * weights[:, column : column + 1]
        )
    return (grad_weight, grad_bias, grad_source)


def shampoo(master, gradient, left_stat, right_stat, left_root, right_root):
    left_new = 0.5 * left_stat + 0.5 * jnp.einsum(
        "kio,kjo->kij", gradient, gradient, precision=highest
    )
    right_new = 0.5 * right_stat + 0.5 * jnp.einsum(
        "kio,kip->kop", gradient, gradient, precision=highest
    )
    direction = jnp.einsum("kij,kjo->kio", left_root, gradient, precision=highest)
    direction = jnp.einsum("kio,kop->kip", direction, right_root, precision=highest)
    updated = master - 1.0 * direction
    return (updated, updated.astype(jnp.bfloat16), left_new, right_new)


def adamw(bias_row, gradient, moment_a, moment_b, step_count):
    first_new = 0.9 * moment_a + 0.1 * gradient
    second_new = 0.95 * moment_b + 0.05 * gradient * gradient
    stepped = step_count.astype(jnp.float32)
    first_hat = first_new / (1.0 - 0.9**stepped)
    second_hat = second_new / (1.0 - 0.95**stepped)
    bias_new = bias_row - 0.1 * (first_hat / (jnp.sqrt(second_hat) + 1e-08) + 0.01 * bias_row)
    return (bias_new, first_new, second_new)


def body(
    features,
    requests,
    adjacent_one,
    adjacent_two,
    adjacent_three,
    valid_one,
    valid_two,
    valid_three,
    labels,
    labelled,
    weights_in,
    weights_mid,
    weights_out,
    biases,
    moment_one,
    moment_two,
    step_count,
    left_in,
    left_mid,
    left_out,
    right_in,
    right_mid,
    right_out,
    invleft_in,
    invleft_mid,
    invleft_out,
    invright_in,
    invright_mid,
    invright_out,
):
    pulled = pull_features(features, requests)
    masters = (weights_in, weights_mid, weights_out)
    lowered = [item.astype(jnp.bfloat16) for item in masters]
    widths = [item.shape[2] for item in masters]
    offsets = [0, widths[0], widths[0] + widths[1]]
    bias_rows = [biases[offsets[which] : offsets[which] + widths[which]] for which in range(3)]
    links = ((adjacent_one, valid_one), (adjacent_two, valid_two), (adjacent_three, valid_three))
    sources = [pulled]
    mixes = []
    preacts = []
    for layer_num in range(3):
        preact, mixed = forward_layer(
            sources[-1],
            links[layer_num][0],
            links[layer_num][1],
            lowered[layer_num],
            bias_rows[layer_num],
        )
        mixes.append(mixed)
        preacts.append(preact)
        if layer_num < 2:
            sources.append(jax.nn.silu(preact).astype(jnp.bfloat16))
    marked = labelled.astype(jnp.float32)
    log_total = jax.nn.logsumexp(preact, axis=1)
    onehot = (labels[:, None] == jnp.arange(preact.shape[1], dtype=jnp.int32)[None, :]).astype(
        jnp.float32
    )
    picked = jnp.sum(preact * onehot, axis=1)
    loss_sum = jnp.sum(marked * (log_total - picked))
    grad_pre = (marked[:, None] * (jnp.exp(preact - log_total[:, None]) - onehot)).astype(
        jnp.bfloat16
    )
    grad_weights = [None, None, None]
    grad_biases = [None, None, None]
    for layer_num in (2, 1, 0):
        grad_weight, grad_bias, grad_source = backward_layer(
            grad_pre,
            sources[layer_num],
            links[layer_num][0],
            links[layer_num][1],
            mixes[layer_num],
            lowered[layer_num],
            layer_num > 0,
        )
        grad_weights[layer_num] = grad_weight
        grad_biases[layer_num] = grad_bias
        if layer_num > 0:
            grad_pre = (grad_source * silu_slope(preacts[layer_num - 1])).astype(jnp.bfloat16)
    local_count = jnp.sum(marked)
    grad_in, grad_mid, grad_out, grad_bias_all, loss_total, counted = lax.psum(
        (
            grad_weights[0],
            grad_weights[1],
            grad_weights[2],
            jnp.concatenate(grad_biases),
            loss_sum,
            local_count,
        ),
        ("hst", "dev"),
    )
    loss = loss_total / counted
    out_in = shampoo(weights_in, grad_in / counted, left_in, right_in, invleft_in, invright_in)
    out_mid = shampoo(
        weights_mid, grad_mid / counted, left_mid, right_mid, invleft_mid, invright_mid
    )
    out_out = shampoo(
        weights_out, grad_out / counted, left_out, right_out, invleft_out, invright_out
    )
    bias_new, first_new, second_new = adamw(
        biases, grad_bias_all / counted, moment_one, moment_two, step_count
    )
    return (
        loss,
        out_in[0],
        out_mid[0],
        out_out[0],
        out_in[1],
        out_mid[1],
        out_out[1],
        out_in[2],
        out_mid[2],
        out_out[2],
        out_in[3],
        out_mid[3],
        out_out[3],
        bias_new,
        first_new,
        second_new,
    )


def solution(mesh):
    placed = (
        P(("hst", "dev"), None),
        P(("hst", "dev"), None),
        P(("hst", "dev"), None),
        P(("hst", "dev"), None),
        P(("hst", "dev"), None),
        P(("hst", "dev"), None),
        P(("hst", "dev"), None),
        P(("hst", "dev"), None),
        P(("hst", "dev")),
        P(("hst", "dev")),
        P(),
        P(),
        P(),
        P(),
        P(),
        P(),
        P(),
        P(),
        P(),
        P(),
        P(),
        P(),
        P(),
        P(),
        P(),
        P(),
        P(),
        P(),
        P(),
    )
    return jax.shard_map(
        body,
        mesh=mesh,
        in_specs=placed,
        out_specs=(P(), P(), P(), P(), P(), P(), P(), P(), P(), P(), P(), P(), P(), P(), P(), P()),
        check_vma=False,
    )
```

profile of v0, /device:TPU:0, one launch (start us, length us, event | category | flops | bytes accessed | tf_op | source)
XLA Modules:
  0.0 596.0 jit_solution(15780768578314852755)
XLA Ops:
  7.2 1.5 all_to_all.11
  8.6 7.3 %all-to-all-start = ((s32[32,1,256]{2,1,0:T(1,128)}), s32[32,1,256]{2,1,0:T(1,128)S(1)}, u32[]{:S(2)}, u32[]{:S(2)}) async-start(s32[32,1,256]{2,1,0:T(1,128)} %all_to_all.11), calls=%async_computation | async-start | bytes 65536 | tf_op jit(solution)/shard_map/all_to_all | solution.py:12
  24.1 1.7 convert_element_type.168
  25.8 31.4 %gather_fusion = bf16[8192,128]{1,0:T(8,128)(2,1)} fusion(f32[16384,128]{1,0:T(8,128)} %param.33, s32[8192]{0:T(1024)S(1)} %broadcast_clamp_fusion), kind=kCustom, calls=%fused_computation | custom fusion | bytes 4227072 | tf_op jit(solution)/shard_map/gather | solution.py:11
  57.2 5.8 all-to-all-start.1
  68.3 3.2 fusion.66
  76.5 1.7 slice_reduce_fusion.24
  78.3 2.8 slice_reduce_fusion.14
  83.9 29.2 %all-to-all-done.1 = bf16[32,256,128]{2,1,0:T(8,128)(2,1)S(1)} async-done(((bf16[32,256,128]{2,1,0:T(8,128)(2,1)}), bf16[32,256,128]{2,1,0:T(8,128)(2,1)S(1)}, u32[]{:S(2)}, u32[]{:S(2)}) %all-to-all-start.1) | async-done | bytes 2097184 | tf_op jit(solution)/shard_map/all_to_all | solution.py:14
  113.1 10.5 %gather_fusion.15 = bf16[4224,128]{1,0:T(8,128)(2,1)} fusion(bf16[8192,128]{1,0:T(8,128)(2,1)S(1)} %bitcast.89, s32[5120]{0:T(1024)} %get-tuple-element.182), kind=kCustom, calls=%fused_computation.15 | custom fusion | bytes 2179584 | tf_op jit(solution)/shard_map/gather | solution.py:29
  123.7 10.5 %gather_fusion.14 = bf16[4224,128]{1,0:T(8,128)(2,1)} fusion(bf16[8192,128]{1,0:T(8,128)(2,1)S(1)} %bitcast.90, s32[5120]{0:T(1024)} %get-tuple-element.183), kind=kCustom, calls=%fused_computation.14 | custom fusion | bytes 2179584 | tf_op jit(solution)/shard_map/gather | solution.py:29
  134.2 9.6 %gather_fusion.13 = bf16[4224,128]{1,0:T(8,128)(2,1)} fusion(bf16[8192,128]{1,0:T(8,128)(2,1)S(1)} %bitcast.91, s32[5120]{0:T(1024)S(1)} %copy-done.25), kind=kCustom, calls=%fused_computation.13 | custom fusion | bytes 2179584 | tf_op jit(solution)/shard_map/gather | solution.py:29
  143.8 9.6 %gather_fusion.12 = bf16[4224,128]{1,0:T(8,128)(2,1)} fusion(bf16[8192,128]{1,0:T(8,128)(2,1)S(1)} %bitcast.92, s32[5120]{0:T(1024)S(1)} %get-tuple-element.185), kind=kCustom, calls=%fused_computation.12 | custom fusion | bytes 2179584 | tf_op jit(solution)/shard_map/gather | solution.py:29
  153.4 10.5 %gather_fusion.11 = bf16[4224,128]{1,0:T(8,128)(2,1)} fusion(bf16[8192,128]{1,0:T(8,128)(2,1)S(1)} %bitcast.93, s32[5120]{0:T(1024)} %get-tuple-element.186), kind=kCustom, calls=%fused_computation.11 | custom fusion | bytes 2179584 | tf_op jit(solution)/shard_map/gather | solution.py:29
  163.9 9.6 %gather_fusion.10 = bf16[4224,128]{1,0:T(8,128)(2,1)} fusion(bf16[8192,128]{1,0:T(8,128)(2,1)S(1)} %bitcast.94, s32[5120]{0:T(1024)S(1)} %copy-done.20), kind=kCustom, calls=%fused_computation.10 | custom fusion | bytes 2179584 | tf_op jit(solution)/shard_map/gather | solution.py:29
  173.5 9.6 %gather_fusion.9 = bf16[4224,128]{1,0:T(8,128)(2,1)} fusion(bf16[8192,128]{1,0:T(8,128)(2,1)S(1)} %bitcast.95, s32[5120]{0:T(1024)S(1)} %copy-done.26), kind=kCustom, calls=%fused_computation.9 | custom fusion | bytes 2179584 | tf_op jit(solution)/shard_map/gather | solution.py:29
  183.0 9.6 %gather_fusion.8 = bf16[4224,128]{1,0:T(8,128)(2,1)} fusion(bf16[8192,128]{1,0:T(8,128)(2,1)S(1)} %bitcast.96, s32[5120]{0:T(1024)S(1)} %copy-done.21), kind=kCustom, calls=%fused_computation.8 | custom fusion | bytes 2179584 | tf_op jit(solution)/shard_map/gather | solution.py:29
  192.6 9.5 %gather_fusion.7 = bf16[4224,128]{1,0:T(8,128)(2,1)} fusion(bf16[8192,128]{1,0:T(8,128)(2,1)S(1)} %bitcast.97, s32[5120]{0:T(1024)S(1)} %copy-done.27), kind=kCustom, calls=%fused_computation.7 | custom fusion | bytes 2179584 | tf_op jit(solution)/shard_map/gather | solution.py:29
  202.2 9.6 %gather_fusion.6 = bf16[4224,128]{1,0:T(8,128)(2,1)} fusion(bf16[8192,128]{1,0:T(8,128)(2,1)S(1)} %bitcast.98, s32[5120]{0:T(1024)S(1)} %copy-done.22), kind=kCustom, calls=%fused_computation.6 | custom fusion | bytes 2179584 | tf_op jit(solution)/shard_map/gather | solution.py:29
  211.8 9.6 %gather_fusion.5 = bf16[4224,128]{1,0:T(8,128)(2,1)} fusion(bf16[8192,128]{1,0:T(8,128)(2,1)S(1)} %bitcast.99, s32[5120]{0:T(1024)S(1)} %copy-done.28), kind=kCustom, calls=%fused_computation.5 | custom fusion | bytes 2179584 | tf_op jit(solution)/shard_map/gather | solution.py:29
  221.4 9.6 %gather_fusion.4 = bf16[4224,128]{1,0:T(8,128)(2,1)} fusion(bf16[8192,128]{1,0:T(8,128)(2,1)S(1)} %bitcast.100, s32[5120]{0:T(1024)S(1)} %copy-done.23), kind=kCustom, calls=%fused_computation.4 | custom fusion | bytes 2179584 | tf_op jit(solution)/shard_map/gather | solution.py:29
  231.0 9.6 %gather_fusion.3 = bf16[4224,128]{1,0:T(8,128)(2,1)} fusion(bf16[8192,128]{1,0:T(8,128)(2,1)S(1)} %bitcast.101, s32[5120]{0:T(1024)S(1)} %copy-done.29), kind=kCustom, calls=%fused_computation.3 | custom fusion | bytes 2179584 | tf_op jit(solution)/shard_map/gather | solution.py:29
  240.5 9.6 %gather_fusion.2 = bf16[4224,128]{1,0:T(8,128)(2,1)} fusion(bf16[8192,128]{1,0:T(8,128)(2,1)S(1)} %bitcast.102, s32[5120]{0:T(1024)S(1)} %copy-done.24), kind=kCustom, calls=%fused_computation.2 | custom fusion | bytes 2179584 | tf_op jit(solution)/shard_map/gather | solution.py:29
  250.1 9.6 %gather_fusion.1 = bf16[4224,128]{1,0:T(8,128)(2,1)} fusion(bf16[8192,128]{1,0:T(8,128)(2,1)S(1)} %bitcast.103, s32[5120]{0:T(1024)S(1)} %copy-done.30), kind=kCustom, calls=%fused_computation.1 | custom fusion | bytes 2179584 | tf_op jit(solution)/shard_map/gather | solution.py:29
  262.2 13.4 %divide_convert_fusion = bf16[4224,128]{1,0:T(8,128)(2,1)S(1)} fusion(bf16[4224,128]{1,0:T(8,128)(2,1)S(1)} %copy-done.1, bf16[4224,128]{1,0:T(8,128)(2,1)S(1)} %copy-done.2, bf16[4224,128]{1,0:T(8,128)(2,1)S(1)} %copy-done.3, bf16[4224,128]{1,0:T(8,128)(2,1)S(1)} %copy-done.4, bf16[4224,128]{1,0:T(8,128)(2,1)S(1)} %copy-done.5, ...), kind=kLoop, calls=%fused_computation.52 | loop fusion | flops 24870912 | bytes 17571840 | tf_op jit(solution)/shard_map/convert_element_type | solution.py:31
  275.7 4.0 multiply_convert_fusion.1
  279.7 3.6 gather_fusion.25
  283.3 4.1 gather_fusion.24
  287.3 4.1 gather_fusion.23
  291.4 4.2 gather_fusion.22
  295.7 4.1 gather_fusion.21
  299.7 4.1 gather_fusion.20
  303.8 4.1 gather_fusion.19
  307.9 4.1 gather_fusion.18
  312.0 4.1 gather_fusion.17
  316.1 4.1 gather_fusion.16
  321.4 2.1 divide_convert_fusion.1
  326.1 1.4 gather_fusion.28
  327.6 1.4 gather_fusion.27
  329.0 1.4 gather_fusion.26
  344.7 1.7 convert_reduce_fusion.1
  346.4 1.9 convolution_bitcast_fusion.1
  348.3 1.9 convolution_bitcast_fusion
  351.4 2.3 scatter-add.121
  353.6 7.3 %scatter_custom_fusion.5 = f32[4224,256]{1,0:T(8,128)} fusion(f32[4224,256]{1,0:T(8,128)} %scatter-add.121, s32[384]{0:T(512)} %copy-done.68, f32[384,256]{1,0:T(8,128)S(1)} %convolution_divide_fusion, f32[384]{0:T(512)S(1)} %copy-done.42), kind=kCustom, calls=%fused_computation.103 | custom fusion | flops 196608 | bytes 4720128 | tf_op jit(solution)/shard_map/scatter-add | solution.py:70
  360.9 6.9 %scatter_custom_fusion.6 = f32[4224,256]{1,0:T(8,128)} fusion(f32[4224,256]{1,0:T(8,128)} %scatter_custom_fusion.5, s32[384]{0:T(512)} %copy-done.67, f32[384,256]{1,0:T(8,128)S(1)} %convolution_divide_fusion, f32[384]{0:T(512)S(1)} %copy-done.40), kind=kCustom, calls=%fused_computation.101 | custom fusion | flops 196608 | bytes 4720128 | tf_op jit(solution)/shard_map/scatter-add | solution.py:70
  367.8 6.9 %scatter_custom_fusion.7 = f32[4224,256]{1,0:T(8,128)} fusion(f32[4224,256]{1,0:T(8,128)} %scatter_custom_fusion.6, s32[384]{0:T(512)} %copy-done.66, f32[384,256]{1,0:T(8,128)S(1)} %convolution_divide_fusion, f32[384]{0:T(512)S(1)} %copy-done.38), kind=kCustom, calls=%fused_computation.99 | custom fusion | flops 196608 | bytes 4720128 | tf_op jit(solution)/shard_map/scatter-add | solution.py:70
  374.6 6.9 %scatter_custom_fusion.8 = f32[4224,256]{1,0:T(8,128)} fusion(f32[4224,256]{1,0:T(8,128)} %scatter_custom_fusion.7, s32[384]{0:T(512)} %copy-done.65, f32[384,256]{1,0:T(8,128)S(1)} %convolution_divide_fusion, f32[384]{0:T(512)S(1)} %copy-done.37), kind=kCustom, calls=%fused_computation.97 | custom fusion | flops 196608 | bytes 4720128 | tf_op jit(solution)/shard_map/scatter-add | solution.py:70
  381.5 6.9 %scatter_custom_fusion.9 = f32[4224,256]{1,0:T(8,128)} fusion(f32[4224,256]{1,0:T(8,128)} %scatter_custom_fusion.8, s32[384]{0:T(512)} %copy-done.64, f32[384,256]{1,0:T(8,128)S(1)} %convolution_divide_fusion, f32[384]{0:T(512)S(1)} %copy-done.36), kind=kCustom, calls=%fused_computation.95 | custom fusion | flops 196608 | bytes 4720128 | tf_op jit(solution)/shard_map/scatter-add | solution.py:70
  388.3 6.9 %scatter_custom_fusion.10 = f32[4224,256]{1,0:T(8,128)} fusion(f32[4224,256]{1,0:T(8,128)} %scatter_custom_fusion.9, s32[384]{0:T(512)} %copy-done.63, f32[384,256]{1,0:T(8,128)S(1)} %convolution_divide_fusion, f32[384]{0:T(512)S(1)} %copy-done.35), kind=kCustom, calls=%fused_computation.93 | custom fusion | flops 196608 | bytes 4720128 | tf_op jit(solution)/shard_map/scatter-add | solution.py:70
  395.2 7.0 %scatter_custom_fusion.11 = f32[4224,256]{1,0:T(8,128)} fusion(f32[4224,256]{1,0:T(8,128)} %scatter_custom_fusion.10, s32[384]{0:T(512)} %copy-done.62, f32[384,256]{1,0:T(8,128)S(1)} %convolution_divide_fusion, f32[384]{0:T(512)S(1)} %copy-done.34), kind=kCustom, calls=%fused_computation.91 | custom fusion | flops 196608 | bytes 4720128 | tf_op jit(solution)/shard_map/scatter-add | solution.py:70
  402.2 6.9 %scatter_custom_fusion.12 = f32[4224,256]{1,0:T(8,128)} fusion(f32[4224,256]{1,0:T(8,128)} %scatter_custom_fusion.11, s32[384]{0:T(512)} %copy-done.61, f32[384,256]{1,0:T(8,128)S(1)} %convolution_divide_fusion, f32[384]{0:T(512)S(1)} %copy-done.33), kind=kCustom, calls=%fused_computation.89 | custom fusion | flops 196608 | bytes 4720128 | tf_op jit(solution)/shard_map/scatter-add | solution.py:70
  409.0 6.9 %scatter_custom_fusion.13 = f32[4224,256]{1,0:T(8,128)} fusion(f32[4224,256]{1,0:T(8,128)} %scatter_custom_fusion.12, s32[384]{0:T(512)} %copy-done.60, f32[384,256]{1,0:T(8,128)S(1)} %convolution_divide_fusion, f32[384]{0:T(512)S(1)} %copy-done.32), kind=kCustom, calls=%fused_computation.87 | custom fusion | flops 196608 | bytes 4720128 | tf_op jit(solution)/shard_map/scatter-add | solution.py:70
  415.9 6.9 %scatter_custom_fusion.14 = f32[4224,256]{1,0:T(8,128)} fusion(f32[4224,256]{1,0:T(8,128)} %scatter_custom_fusion.13, s32[384]{0:T(512)} %copy-done.59, f32[384,256]{1,0:T(8,128)S(1)} %convolution_divide_fusion, f32[384]{0:T(512)S(1)} %get-tuple-element.121), kind=kCustom, calls=%fused_computation.85 | custom fusion | flops 196608 | bytes 4720128 | tf_op jit(solution)/shard_map/scatter-add | solution.py:70
  422.7 4.4 convert_reduce_fusion
  432.5 37.9 %all-reduce.2 = (f32[]{:T(128)}, f32[]{:T(128)}, f32[684]{0:T(1024)S(1)}) all-reduce(f32[]{:T(128)} %get-tuple-element.141, f32[]{:T(128)} %get-tuple-element.140, f32[684]{0:T(1024)S(1)} %pad_maximum_fusion.3), channel_id=1, replica_groups=mesh['hst'=4,'dev'=8] {'hst','dev'}, use_global_device_ids=true, to_apply=%region_7.8 | all-reduce | flops 686 | bytes 5488 | tf_op jit(solution)/shard_map/psum | solution.py:179
  473.0 88.9 %all-reduce.6.cloned.1.call-done = (f32[2,128,256]{2,1,0:T(8,128)}, f32[2,256,256]{2,1,0:T(8,128)}, f32[2,256,172]{1,2,0:T(8,128)}) async-done(((f32[2,128,256]{2,1,0:T(8,128)}, f32[2,256,256]{2,1,0:T(8,128)}, f32[2,256,172]{1,2,0:T(8,128)}), (f32[2,128,256]{2,1,0:T(8,128)}, f32[2,256,256]{2,1,0:T(8,128)}, f32[2,256,172]{1,2,0:T(8,128)})) %all-reduce.6.cloned.1.call-update) | async-done | bytes 1138704 | tf_op jit(solution)/shard_map/psum | solution.py:179
  561.9 2.8 fusion.7
  564.7 2.1 fusion.97
  566.8 3.2 fusion.3
  573.6 2.6 fusion.4
  578.9 2.6 fusion.1
  581.5 2.2 fusion.2
  586.3 1.5 fusion.104
  (257 shorter events, 57.4 us)
Async XLA Ops:
  7.2 579.1 %copy-start = (f32[2,256,256]{2,1,0:T(8,128)S(1)}, f32[2,256,256]{2,1,0:T(8,128)}, u32[]{:S(2)}) copy-start(f32[2,256,256]{2,1,0:T(8,128)} %param.60) | copy-start | bytes 1572868
  8.6 17.1 %all-to-all-start = ((s32[32,1,256]{2,1,0:T(1,128)}), s32[32,1,256]{2,1,0:T(1,128)S(1)}, u32[]{:S(2)}, u32[]{:S(2)}) async-start(s32[32,1,256]{2,1,0:T(1,128)} %all_to_all.11), calls=%async_computation | async-start | bytes 65536 | tf_op jit(solution)/shard_map/all_to_all | solution.py:12
  57.2 5.9 copy-start.78
  57.2 6.6 %copy-start.43 = (s32[64,5]{0,1:T(8,128)S(1)}, s32[64,5]{0,1:T(8,128)}, u32[]{:S(2)}) copy-start(s32[64,5]{0,1:T(8,128)} %param.40) | copy-start | bytes 3844
  57.2 7.9 %copy-start.47 = (s32[384,10]{0,1:T(8,128)S(1)}, s32[384,10]{0,1:T(8,128)}, u32[]{:S(2)}) copy-start(s32[384,10]{0,1:T(8,128)} %param.36) | copy-start | bytes 46084
  57.2 15.0 %copy-start.19 = (s32[384,10]{0,1:T(8,128)S(1)}, s32[384,10]{0,1:T(8,128)}, u32[]{:S(2)}) copy-start(s32[384,10]{0,1:T(8,128)} %param.39) | copy-start | bytes 46084
  57.2 21.0 %copy-start.10 = (s32[4224,15]{0,1:T(8,128)S(1)}, s32[4224,15]{0,1:T(8,128)}, u32[]{:S(2)}) copy-start(s32[4224,15]{0,1:T(8,128)} %param.38) | copy-start | bytes 760324
  57.2 55.9 %all-to-all-start.1 = ((bf16[32,256,128]{2,1,0:T(8,128)(2,1)}), bf16[32,256,128]{2,1,0:T(8,128)(2,1)S(1)}, u32[]{:S(2)}, u32[]{:S(2)}) async-start(bf16[32,256,128]{2,1,0:T(8,128)(2,1)} %bitcast.106), calls=%async_computation.1 | async-start | bytes 4194304 | tf_op jit(solution)/shard_map/all_to_all | solution.py:14
  63.1 498.9 %all-reduce.6.cloned.1.call-start = ((), (), s32[]{:S(2)}) async-start(), calls=%async_computation.2 | async-start | bytes 2293760 | tf_op jit(solution)/shard_map/psum | solution.py:179
  63.1 19.0 %copy-start.44 = (f32[684]{0:T(1024)S(1)}, f32[684]{0:T(1024)}, u32[]{:S(2)}) copy-start(f32[684]{0:T(1024)} %param.46) | copy-start | bytes 8212
  63.1 19.6 %copy-start.46 = (f32[64,5]{0,1:T(8,128)S(1)}, f32[64,5]{0,1:T(8,128)}, u32[]{:S(2)}) copy-start(f32[64,5]{0,1:T(8,128)} %convert_element_type.201) | copy-start | bytes 3844
  123.7 10.5 %copy-start.25 = (s32[5120]{0:T(1024)S(1)}, s32[5120]{0:T(1024)}, u32[]{:S(2)}) copy-start(s32[5120]{0:T(1024)} %get-tuple-element.184) | copy-start | bytes 61444
  153.4 10.5 %copy-start.20 = (s32[5120]{0:T(1024)S(1)}, s32[5120]{0:T(1024)}, u32[]{:S(2)}) copy-start(s32[5120]{0:T(1024)} %get-tuple-element.187) | copy-start | bytes 61444
  163.9 9.6 %copy-start.26 = (s32[5120]{0:T(1024)S(1)}, s32[5120]{0:T(1024)}, u32[]{:S(2)}) copy-start(s32[5120]{0:T(1024)} %get-tuple-element.188) | copy-start | bytes 61444
  173.5 9.6 %copy-start.21 = (s32[5120]{0:T(1024)S(1)}, s32[5120]{0:T(1024)}, u32[]{:S(2)}) copy-start(s32[5120]{0:T(1024)} %get-tuple-element.189) | copy-start | bytes 61444
  183.0 9.6 %copy-start.27 = (s32[5120]{0:T(1024)S(1)}, s32[5120]{0:T(1024)}, u32[]{:S(2)}) copy-start(s32[5120]{0:T(1024)} %get-tuple-element.190) | copy-start | bytes 61444
  192.6 9.6 %copy-start.22 = (s32[5120]{0:T(1024)S(1)}, s32[5120]{0:T(1024)}, u32[]{:S(2)}) copy-start(s32[5120]{0:T(1024)} %get-tuple-element.191) | copy-start | bytes 61444
  202.2 9.6 %copy-start.28 = (s32[5120]{0:T(1024)S(1)}, s32[5120]{0:T(1024)}, u32[]{:S(2)}) copy-start(s32[5120]{0:T(1024)} %get-tuple-element.192) | copy-start | bytes 61444
  211.8 9.6 %copy-start.23 = (s32[5120]{0:T(1024)S(1)}, s32[5120]{0:T(1024)}, u32[]{:S(2)}) copy-start(s32[5120]{0:T(1024)} %get-tuple-element.193) | copy-start | bytes 61444
  221.4 9.6 %copy-start.29 = (s32[5120]{0:T(1024)S(1)}, s32[5120]{0:T(1024)}, u32[]{:S(2)}) copy-start(s32[5120]{0:T(1024)} %get-tuple-element.194) | copy-start | bytes 61444
  231.0 9.6 %copy-start.24 = (s32[5120]{0:T(1024)S(1)}, s32[5120]{0:T(1024)}, u32[]{:S(2)}) copy-start(s32[5120]{0:T(1024)} %get-tuple-element.195) | copy-start | bytes 61444
  240.5 9.6 %copy-start.30 = (s32[5120]{0:T(1024)S(1)}, s32[5120]{0:T(1024)}, u32[]{:S(2)}) copy-start(s32[5120]{0:T(1024)} %pad_clamp_fusion.14) | copy-start | bytes 61444
  275.6 4.0 copy-start.6
  275.6 4.0 copy-start.57
  275.6 7.6 %copy-start.56 = (s32[1024]{0:T(1024)S(1)}, s32[1024]{0:T(1024)}, u32[]{:S(2)}) copy-start(s32[1024]{0:T(1024)} %get-tuple-element.197) | copy-start | bytes 12292
  279.7 7.7 %copy-start.55 = (s32[1024]{0:T(1024)S(1)}, s32[1024]{0:T(1024)}, u32[]{:S(2)}) copy-start(s32[1024]{0:T(1024)} %get-tuple-element.198) | copy-start | bytes 12292
  283.3 8.2 %copy-start.54 = (s32[1024]{0:T(1024)S(1)}, s32[1024]{0:T(1024)}, u32[]{:S(2)}) copy-start(s32[1024]{0:T(1024)} %get-tuple-element.199) | copy-start | bytes 12292
  287.3 8.3 %copy-start.53 = (s32[1024]{0:T(1024)S(1)}, s32[1024]{0:T(1024)}, u32[]{:S(2)}) copy-start(s32[1024]{0:T(1024)} %get-tuple-element.200) | copy-start | bytes 12292
  291.4 8.3 %copy-start.52 = (s32[1024]{0:T(1024)S(1)}, s32[1024]{0:T(1024)}, u32[]{:S(2)}) copy-start(s32[1024]{0:T(1024)} %get-tuple-element.201) | copy-start | bytes 12292
  295.7 8.2 %copy-start.51 = (s32[1024]{0:T(1024)S(1)}, s32[1024]{0:T(1024)}, u32[]{:S(2)}) copy-start(s32[1024]{0:T(1024)} %get-tuple-element.202) | copy-start | bytes 12292
  299.7 8.1 %copy-start.50 = (s32[1024]{0:T(1024)S(1)}, s32[1024]{0:T(1024)}, u32[]{:S(2)}) copy-start(s32[1024]{0:T(1024)} %get-tuple-element.203) | copy-start | bytes 12292
  303.8 8.2 %copy-start.49 = (s32[1024]{0:T(1024)S(1)}, s32[1024]{0:T(1024)}, u32[]{:S(2)}) copy-start(s32[1024]{0:T(1024)} %get-tuple-element.204) | copy-start | bytes 12292
  307.9 8.2 %copy-start.48 = (s32[1024]{0:T(1024)S(1)}, s32[1024]{0:T(1024)}, u32[]{:S(2)}) copy-start(s32[1024]{0:T(1024)} %get-tuple-element.205) | copy-start | bytes 12292
  311.9 9.3 %copy-start.32 = (f32[384]{0:T(512)S(1)}, f32[384]{0:T(512)}, u32[]{:S(2)}) copy-start(f32[384]{0:T(512)} %get-tuple-element.122) | copy-start | bytes 4612
  311.9 9.4 %copy-start.33 = (f32[384]{0:T(512)S(1)}, f32[384]{0:T(512)}, u32[]{:S(2)}) copy-start(f32[384]{0:T(512)} %get-tuple-element.123) | copy-start | bytes 4612
  311.9 9.4 %copy-start.34 = (f32[384]{0:T(512)S(1)}, f32[384]{0:T(512)}, u32[]{:S(2)}) copy-start(f32[384]{0:T(512)} %get-tuple-element.124) | copy-start | bytes 4612
  311.9 9.4 %copy-start.35 = (f32[384]{0:T(512)S(1)}, f32[384]{0:T(512)}, u32[]{:S(2)}) copy-start(f32[384]{0:T(512)} %get-tuple-element.125) | copy-start | bytes 4612
  311.9 9.4 %copy-start.36 = (f32[384]{0:T(512)S(1)}, f32[384]{0:T(512)}, u32[]{:S(2)}) copy-start(f32[384]{0:T(512)} %get-tuple-element.126) | copy-start | bytes 4612
  312.0 9.4 %copy-start.37 = (f32[384]{0:T(512)S(1)}, f32[384]{0:T(512)}, u32[]{:S(2)}) copy-start(f32[384]{0:T(512)} %get-tuple-element.127) | copy-start | bytes 4612
  312.0 9.4 %copy-start.38 = (f32[384]{0:T(512)S(1)}, f32[384]{0:T(512)}, u32[]{:S(2)}) copy-start(f32[384]{0:T(512)} %get-tuple-element.128) | copy-start | bytes 4612
  312.0 9.4 %copy-start.39 = (f32[384]{0:T(512)S(1)}, f32[384]{0:T(512)}, u32[]{:S(2)}) copy-start(f32[384]{0:T(512)} %get-tuple-element.129) | copy-start | bytes 4612
  312.0 9.4 %copy-start.41 = (f32[384]{0:T(512)S(1)}, f32[384]{0:T(512)}, u32[]{:S(2)}) copy-start(f32[384]{0:T(512)} %get-tuple-element.120) | copy-start | bytes 4612
  312.0 9.4 %copy-start.58 = (f32[384]{0:T(512)S(1)}, f32[384]{0:T(512)}, u32[]{:S(2)}) copy-start(f32[384]{0:T(512)} %broadcast_maximum_fusion.1) | copy-start | bytes 4612
  316.1 7.4 %copy-start.79 = (f32[256]{0:T(256)S(1)}, f32[256]{0:T(256)}, u32[]{:S(2)}) copy-start(f32[256]{0:T(256)} %get-tuple-element.168) | copy-start | bytes 3076
  323.5 9.0 %copy-start.14 = (bf16[384,256]{1,0:T(8,128)(2,1)}, bf16[384,256]{1,0:T(8,128)(2,1)S(1)}, u32[]{:S(2)}) copy-start(bf16[384,256]{1,0:T(8,128)(2,1)S(1)} %divide_convert_fusion.1) | copy-start | bytes 589828
  353.6 7.3 %copy-start.40 = (f32[384]{0:T(512)S(1)}, f32[384]{0:T(512)}, u32[]{:S(2)}) copy-start(f32[384]{0:T(512)} %get-tuple-element.129) | copy-start | bytes 4612
  429.3 42.4 %copy-start.45 = (f32[684]{0:T(1024)S(1)}, f32[684]{0:T(1024)}, u32[]{:S(2)}) copy-start(f32[684]{0:T(1024)} %param.46) | copy-start | bytes 8212
  429.3 42.4 %copy-start.71 = (f32[684]{0:T(1024)S(1)}, f32[684]{0:T(1024)}, u32[]{:S(2)}) copy-start(f32[684]{0:T(1024)} %param.48) | copy-start | bytes 8212
  429.3 42.4 %copy-start.72 = (f32[684]{0:T(1024)S(1)}, f32[684]{0:T(1024)}, u32[]{:S(2)}) copy-start(f32[684]{0:T(1024)} %param.47) | copy-start | bytes 8212
  429.4 132.6 %copy-start.88 = (f32[2,128,128]{2,1,0:T(8,128)S(1)}, f32[2,128,128]{2,1,0:T(8,128)}, u32[]{:S(2)}) copy-start(f32[2,128,128]{2,1,0:T(8,128)} %param.50) | copy-start | bytes 393220
  429.4 135.4 %copy-start.89 = (f32[2,128,128]{2,1,0:T(8,128)S(1)}, f32[2,128,128]{2,1,0:T(8,128)}, u32[]{:S(2)}) copy-start(f32[2,128,128]{2,1,0:T(8,128)} %param.56) | copy-start | bytes 393220
  430.1 136.6 %copy-start.16 = (f32[2,256,256]{2,1,0:T(8,128)S(1)}, f32[2,256,256]{2,1,0:T(8,128)}, u32[]{:S(2)}) copy-start(f32[2,256,256]{2,1,0:T(8,128)} %param.53) | copy-start | bytes 1572868
  431.7 138.3 %copy-start.87 = (f32[2,172,172]{2,0,1:T(2,128)S(1)}, f32[2,172,172]{2,0,1:T(2,128)}, u32[]{:S(2)}) copy-start(f32[2,172,172]{2,0,1:T(2,128)} %param.55) | copy-start | bytes 710020
  561.9 8.1 %copy-start.86 = (f32[2,256,172]{1,2,0:T(8,128)S(1)}, f32[2,256,172]{1,2,0:T(8,128)}, u32[]{:S(2)}) copy-start(f32[2,256,172]{1,2,0:T(8,128)} %get-tuple-element.147) | copy-start | bytes 1056772
  564.7 7.5 %copy-start.80 = (f32[2,256,256]{2,1,0:T(8,128)S(1)}, f32[2,256,256]{2,1,0:T(8,128)}, u32[]{:S(2)}) copy-start(f32[2,256,256]{2,1,0:T(8,128)} %param.58) | copy-start | bytes 1572868
  566.8 6.7 %copy-start.81 = (f32[2,256,256]{2,1,0:T(8,128)S(1)}, f32[2,256,256]{2,1,0:T(8,128)}, u32[]{:S(2)}) copy-start(f32[2,256,256]{2,1,0:T(8,128)} %param.52) | copy-start | bytes 1572868
  571.2 5.0 copy-start.9
  571.2 5.0 copy-start.18
  573.5 5.3 copy-start.82
  573.6 5.3 copy-start.85
  576.2 5.3 copy-start.83
  578.9 4.8 copy-start.84
  581.5 3.6 copy-start.11
  581.5 3.6 copy-start.17
  (29 other events, 60.0 us)
Sparse Core Ops, SparseCore 0:
  431.8 130.0 all-reduce.5
where the time goes:
time: 602 us; the launch traced here: 596 us
  local copies, waits for them, and re-layouts  242 us (40%)
  other arithmetic  128 us (21%)
  waiting for transfers between devices  118 us (20%)
  matrix products  38.9 us (6%)
  blocking collectives  37.9 us (6%)
  between operations  18.5 us (3%)
  starting transfers between devices  13.2 us (2%)
    gather x30, local copies, waits for them, and re-layouts, forward_layer(): source[adjacent[:, column]].astype(jnp.float32)  193 us
    psum x1, waiting for transfers between devices, body(): lax.psum((grad_weights[0], grad_weights[1], grad_weights[2], jnp.concaten...  88.9 us
    scatter-add x15, other arithmetic, backward_layer(): grad_source.at[adjacent[:, column]]  75.7 us
    psum x1, blocking collectives, body(): lax.psum((grad_weights[0], grad_weights[1], grad_weights[2], jnp.concaten...  37.9 us
    gather x1, local copies, waits for them, and re-layouts, pull_features(): features[lax.all_to_all(requests, ('hst', 'dev'), split_axis=0, concat_ax...  31.4 us
    all_to_all x1, waiting for transfers between devices, pull_features(): lax.all_to_all(found, ('hst', 'dev'), split_axis=0, concat_axis=0, tiled=...  29.2 us
    convert_element_type x3, other arithmetic, forward_layer(): mixed = (summed / counts[:, None]).astype(jnp.bfloat16)  16.5 us
  transfers between devices with their start and end apart: 3, of which 2 were waited for; matrix products, arithmetic and copies ran while one was open for 5% of the time, Pallas kernels for 0%

commit v1 on v0

--- a/solution.py
+++ b/solution.py
@@ -177,15 +177,18 @@
             grad_pre = (grad_source * silu_slope(preacts[layer_num - 1])).astype(jnp.bfloat16)
     local_count = jnp.sum(marked)
     grad_in, grad_mid, grad_out, grad_bias_all, loss_total, counted = lax.psum(
-        (
-            grad_weights[0],
-            grad_weights[1],
-            grad_weights[2],
-            jnp.concatenate(grad_biases),
-            loss_sum,
-            local_count,
+        lax.psum(
+            (
+                grad_weights[0],
+                grad_weights[1],
+                grad_weights[2],
+                jnp.concatenate(grad_biases),
+                loss_sum,
+                local_count,
+            ),
+            "hst",
         ),
-        ("hst", "dev"),
+        "dev",
     )
     loss = loss_total / counted
     out_in = shampoo(weights_in, grad_in / counted, left_in, right_in, invleft_in, invright_in)

time: 602 us -> 593 us (0.985)
  blocking collectives: 37.9 us -> 29.4 us
    psum x1, waiting for transfers between devices: 88.9 us -> 35.3 us  [body(): lax.psum((grad_weights[0], grad_weights[1], grad_weights[2], jnp.concaten...]
    psum x0 -> x1, waiting for transfers between devices: none -> 52.1 us  [body(): lax.psum(lax.psum((grad_weights[0], grad_weights[1], grad_weights[2], jnp...]
    psum x1, blocking collectives: 37.9 us -> 6.82 us  [body(): lax.psum((grad_weights[0], grad_weights[1], grad_weights[2], jnp.concaten...]
    psum x0 -> x1, blocking collectives: none -> 22.6 us  [body(): lax.psum(lax.psum((grad_weights[0], grad_weights[1], grad_weights[2], jnp...]
  transfers between devices with their start and end apart: 3 -> 4, of which waited for: 2 -> 3; matrix products, arithmetic and copies ran while one was open for 5% -> 5% of each run, Pallas kernels for 0% -> 0%
where the time goes in v1:
time: 593 us; the launch traced here: 586 us
  local copies, waits for them, and re-layouts  242 us (41%)
  other arithmetic  128 us (22%)
  waiting for transfers between devices  117 us (20%)
  matrix products  38.9 us (7%)
  blocking collectives  29.4 us (5%)
  between operations  18.5 us (3%)
  starting transfers between devices  13.2 us (2%)
    gather x30, local copies, waits for them, and re-layouts, forward_layer(): source[adjacent[:, column]].astype(jnp.float32)  193 us
    scatter-add x15, other arithmetic, backward_layer(): grad_source.at[adjacent[:, column]]  75.7 us
    psum x1, waiting for transfers between devices, body(): lax.psum(lax.psum((grad_weights[0], grad_weights[1], grad_weights[2], jnp...  52.1 us
    psum x1, waiting for transfers between devices, body(): lax.psum((grad_weights[0], grad_weights[1], grad_weights[2], jnp.concaten...  35.3 us
    gather x1, local copies, waits for them, and re-layouts, pull_features(): features[lax.all_to_all(requests, ('hst', 'dev'), split_axis=0, concat_ax...  31.4 us
    all_to_all x1, waiting for transfers between devices, pull_features(): lax.all_to_all(found, ('hst', 'dev'), split_axis=0, concat_axis=0, tiled=...  29.2 us
    psum x1, blocking collectives, body(): lax.psum(lax.psum((grad_weights[0], grad_weights[1], grad_weights[2], jnp...  22.6 us
    convert_element_type x3, other arithmetic, forward_layer(): mixed = (summed / counts[:, None]).astype(jnp.bfloat16)  16.5 us
  transfers between devices with their start and end apart: 4, of which 3 were waited for; matrix products, arithmetic and copies ran while one was open for 5% of the time, Pallas kernels for 0%

profile of v1, /device:TPU:0, one launch (start us, length us, event | category | flops | bytes accessed | tf_op | source)
XLA Modules:
  0.0 586.2 jit_solution(13890578351511449130)
XLA Ops:
  7.2 1.5 all_to_all.11
  8.6 7.3 %all-to-all-start = ((s32[32,1,256]{2,1,0:T(1,128)}), s32[32,1,256]{2,1,0:T(1,128)S(1)}, u32[]{:S(2)}, u32[]{:S(2)}) async-start(s32[32,1,256]{2,1,0:T(1,128)} %all_to_all.11), calls=%async_computation | async-start | bytes 65536 | tf_op jit(solution)/shard_map/all_to_all | solution.py:12
  24.1 1.7 convert_element_type.168
  25.8 31.4 %gather_fusion = bf16[8192,128]{1,0:T(8,128)(2,1)} fusion(f32[16384,128]{1,0:T(8,128)} %param.33, s32[8192]{0:T(1024)S(1)} %broadcast_clamp_fusion), kind=kCustom, calls=%fused_computation | custom fusion | bytes 4227072 | tf_op jit(solution)/shard_map/gather | solution.py:11
  57.2 5.8 all-to-all-start.1
  68.3 3.2 fusion.66
  76.5 1.7 slice_reduce_fusion.24
  78.3 2.8 slice_reduce_fusion.14
  83.9 29.2 %all-to-all-done.1 = bf16[32,256,128]{2,1,0:T(8,128)(2,1)S(1)} async-done(((bf16[32,256,128]{2,1,0:T(8,128)(2,1)}), bf16[32,256,128]{2,1,0:T(8,128)(2,1)S(1)}, u32[]{:S(2)}, u32[]{:S(2)}) %all-to-all-start.1) | async-done | bytes 2097184 | tf_op jit(solution)/shard_map/all_to_all | solution.py:14
  113.1 10.5 %gather_fusion.15 = bf16[4224,128]{1,0:T(8,128)(2,1)} fusion(bf16[8192,128]{1,0:T(8,128)(2,1)S(1)} %bitcast.89, s32[5120]{0:T(1024)} %get-tuple-element.188), kind=kCustom, calls=%fused_computation.15 | custom fusion | bytes 2179584 | tf_op jit(solution)/shard_map/gather | solution.py:29
  123.7 10.5 %gather_fusion.14 = bf16[4224,128]{1,0:T(8,128)(2,1)} fusion(bf16[8192,128]{1,0:T(8,128)(2,1)S(1)} %bitcast.90, s32[5120]{0:T(1024)} %get-tuple-element.189), kind=kCustom, calls=%fused_computation.14 | custom fusion | bytes 2179584 | tf_op jit(solution)/shard_map/gather | solution.py:29
  134.2 9.6 %gather_fusion.13 = bf16[4224,128]{1,0:T(8,128)(2,1)} fusion(bf16[8192,128]{1,0:T(8,128)(2,1)S(1)} %bitcast.91, s32[5120]{0:T(1024)S(1)} %copy-done.25), kind=kCustom, calls=%fused_computation.13 | custom fusion | bytes 2179584 | tf_op jit(solution)/shard_map/gather | solution.py:29
  143.8 9.6 %gather_fusion.12 = bf16[4224,128]{1,0:T(8,128)(2,1)} fusion(bf16[8192,128]{1,0:T(8,128)(2,1)S(1)} %bitcast.92, s32[5120]{0:T(1024)S(1)} %get-tuple-element.191), kind=kCustom, calls=%fused_computation.12 | custom fusion | bytes 2179584 | tf_op jit(solution)/shard_map/gather | solution.py:29
  153.4 10.5 %gather_fusion.11 = bf16[4224,128]{1,0:T(8,128)(2,1)} fusion(bf16[8192,128]{1,0:T(8,128)(2,1)S(1)} %bitcast.93, s32[5120]{0:T(1024)} %get-tuple-element.192), kind=kCustom, calls=%fused_computation.11 | custom fusion | bytes 2179584 | tf_op jit(solution)/shard_map/gather | solution.py:29
  163.9 9.6 %gather_fusion.10 = bf16[4224,128]{1,0:T(8,128)(2,1)} fusion(bf16[8192,128]{1,0:T(8,128)(2,1)S(1)} %bitcast.94, s32[5120]{0:T(1024)S(1)} %copy-done.20), kind=kCustom, calls=%fused_computation.10 | custom fusion | bytes 2179584 | tf_op jit(solution)/shard_map/gather | solution.py:29
  173.5 9.6 %gather_fusion.9 = bf16[4224,128]{1,0:T(8,128)(2,1)} fusion(bf16[8192,128]{1,0:T(8,128)(2,1)S(1)} %bitcast.95, s32[5120]{0:T(1024)S(1)} %copy-done.26), kind=kCustom, calls=%fused_computation.9 | custom fusion | bytes 2179584 | tf_op jit(solution)/shard_map/gather | solution.py:29
  183.0 9.6 %gather_fusion.8 = bf16[4224,128]{1,0:T(8,128)(2,1)} fusion(bf16[8192,128]{1,0:T(8,128)(2,1)S(1)} %bitcast.96, s32[5120]{0:T(1024)S(1)} %copy-done.21), kind=kCustom, calls=%fused_computation.8 | custom fusion | bytes 2179584 | tf_op jit(solution)/shard_map/gather | solution.py:29
  192.6 9.5 %gather_fusion.7 = bf16[4224,128]{1,0:T(8,128)(2,1)} fusion(bf16[8192,128]{1,0:T(8,128)(2,1)S(1)} %bitcast.97, s32[5120]{0:T(1024)S(1)} %copy-done.27), kind=kCustom, calls=%fused_computation.7 | custom fusion | bytes 2179584 | tf_op jit(solution)/shard_map/gather | solution.py:29
  202.2 9.6 %gather_fusion.6 = bf16[4224,128]{1,0:T(8,128)(2,1)} fusion(bf16[8192,128]{1,0:T(8,128)(2,1)S(1)} %bitcast.98, s32[5120]{0:T(1024)S(1)} %copy-done.22), kind=kCustom, calls=%fused_computation.6 | custom fusion | bytes 2179584 | tf_op jit(solution)/shard_map/gather | solution.py:29
  211.8 9.6 %gather_fusion.5 = bf16[4224,128]{1,0:T(8,128)(2,1)} fusion(bf16[8192,128]{1,0:T(8,128)(2,1)S(1)} %bitcast.99, s32[5120]{0:T(1024)S(1)} %copy-done.28), kind=kCustom, calls=%fused_computation.5 | custom fusion | bytes 2179584 | tf_op jit(solution)/shard_map/gather | solution.py:29
  221.4 9.6 %gather_fusion.4 = bf16[4224,128]{1,0:T(8,128)(2,1)} fusion(bf16[8192,128]{1,0:T(8,128)(2,1)S(1)} %bitcast.100, s32[5120]{0:T(1024)S(1)} %copy-done.23), kind=kCustom, calls=%fused_computation.4 | custom fusion | bytes 2179584 | tf_op jit(solution)/shard_map/gather | solution.py:29
  231.0 9.6 %gather_fusion.3 = bf16[4224,128]{1,0:T(8,128)(2,1)} fusion(bf16[8192,128]{1,0:T(8,128)(2,1)S(1)} %bitcast.101, s32[5120]{0:T(1024)S(1)} %copy-done.29), kind=kCustom, calls=%fused_computation.3 | custom fusion | bytes 2179584 | tf_op jit(solution)/shard_map/gather | solution.py:29
  240.5 9.6 %gather_fusion.2 = bf16[4224,128]{1,0:T(8,128)(2,1)} fusion(bf16[8192,128]{1,0:T(8,128)(2,1)S(1)} %bitcast.102, s32[5120]{0:T(1024)S(1)} %copy-done.24), kind=kCustom, calls=%fused_computation.2 | custom fusion | bytes 2179584 | tf_op jit(solution)/shard_map/gather | solution.py:29
  250.1 9.6 %gather_fusion.1 = bf16[4224,128]{1,0:T(8,128)(2,1)} fusion(bf16[8192,128]{1,0:T(8,128)(2,1)S(1)} %bitcast.103, s32[5120]{0:T(1024)S(1)} %copy-done.30), kind=kCustom, calls=%fused_computation.1 | custom fusion | bytes 2179584 | tf_op jit(solution)/shard_map/gather | solution.py:29
  262.2 13.4 %divide_convert_fusion = bf16[4224,128]{1,0:T(8,128)(2,1)S(1)} fusion(bf16[4224,128]{1,0:T(8,128)(2,1)S(1)} %copy-done.1, bf16[4224,128]{1,0:T(8,128)(2,1)S(1)} %copy-done.2, bf16[4224,128]{1,0:T(8,128)(2,1)S(1)} %copy-done.3, bf16[4224,128]{1,0:T(8,128)(2,1)S(1)} %copy-done.4, bf16[4224,128]{1,0:T(8,128)(2,1)S(1)} %copy-done.5, ...), kind=kLoop, calls=%fused_computation.52 | loop fusion | flops 24870912 | bytes 17571840 | tf_op jit(solution)/shard_map/convert_element_type | solution.py:31
  275.7 4.0 multiply_convert_fusion.1
  279.7 3.6 gather_fusion.25
  283.3 4.1 gather_fusion.24
  287.3 4.1 gather_fusion.23
  291.4 4.2 gather_fusion.22
  295.7 4.1 gather_fusion.21
  299.7 4.1 gather_fusion.20
  303.8 4.1 gather_fusion.19
  307.9 4.1 gather_fusion.18
  312.0 4.1 gather_fusion.17
  316.1 4.1 gather_fusion.16
  321.4 2.1 divide_convert_fusion.1
  326.1 1.4 gather_fusion.28
  344.7 1.7 convert_reduce_fusion.1
  346.4 1.9 convolution_bitcast_fusion.1
  348.3 1.9 convolution_bitcast_fusion
  351.4 2.3 scatter-add.121
  353.6 7.3 %scatter_custom_fusion.5 = f32[4224,256]{1,0:T(8,128)} fusion(f32[4224,256]{1,0:T(8,128)} %scatter-add.121, s32[384]{0:T(512)} %copy-done.68, f32[384,256]{1,0:T(8,128)S(1)} %convolution_divide_fusion, f32[384]{0:T(512)S(1)} %copy-done.42), kind=kCustom, calls=%fused_computation.103 | custom fusion | flops 196608 | bytes 4720128 | tf_op jit(solution)/shard_map/scatter-add | solution.py:70
  360.9 6.9 %scatter_custom_fusion.6 = f32[4224,256]{1,0:T(8,128)} fusion(f32[4224,256]{1,0:T(8,128)} %scatter_custom_fusion.5, s32[384]{0:T(512)} %copy-done.67, f32[384,256]{1,0:T(8,128)S(1)} %convolution_divide_fusion, f32[384]{0:T(512)S(1)} %copy-done.40), kind=kCustom, calls=%fused_computation.101 | custom fusion | flops 196608 | bytes 4720128 | tf_op jit(solution)/shard_map/scatter-add | solution.py:70
  367.8 6.9 %scatter_custom_fusion.7 = f32[4224,256]{1,0:T(8,128)} fusion(f32[4224,256]{1,0:T(8,128)} %scatter_custom_fusion.6, s32[384]{0:T(512)} %copy-done.66, f32[384,256]{1,0:T(8,128)S(1)} %convolution_divide_fusion, f32[384]{0:T(512)S(1)} %copy-done.38), kind=kCustom, calls=%fused_computation.99 | custom fusion | flops 196608 | bytes 4720128 | tf_op jit(solution)/shard_map/scatter-add | solution.py:70
  374.6 6.9 %scatter_custom_fusion.8 = f32[4224,256]{1,0:T(8,128)} fusion(f32[4224,256]{1,0:T(8,128)} %scatter_custom_fusion.7, s32[384]{0:T(512)} %copy-done.65, f32[384,256]{1,0:T(8,128)S(1)} %convolution_divide_fusion, f32[384]{0:T(512)S(1)} %copy-done.37), kind=kCustom, calls=%fused_computation.97 | custom fusion | flops 196608 | bytes 4720128 | tf_op jit(solution)/shard_map/scatter-add | solution.py:70
  381.5 6.9 %scatter_custom_fusion.9 = f32[4224,256]{1,0:T(8,128)} fusion(f32[4224,256]{1,0:T(8,128)} %scatter_custom_fusion.8, s32[384]{0:T(512)} %copy-done.64, f32[384,256]{1,0:T(8,128)S(1)} %convolution_divide_fusion, f32[384]{0:T(512)S(1)} %copy-done.36), kind=kCustom, calls=%fused_computation.95 | custom fusion | flops 196608 | bytes 4720128 | tf_op jit(solution)/shard_map/scatter-add | solution.py:70
  388.3 6.9 %scatter_custom_fusion.10 = f32[4224,256]{1,0:T(8,128)} fusion(f32[4224,256]{1,0:T(8,128)} %scatter_custom_fusion.9, s32[384]{0:T(512)} %copy-done.63, f32[384,256]{1,0:T(8,128)S(1)} %convolution_divide_fusion, f32[384]{0:T(512)S(1)} %copy-done.35), kind=kCustom, calls=%fused_computation.93 | custom fusion | flops 196608 | bytes 4720128 | tf_op jit(solution)/shard_map/scatter-add | solution.py:70
  395.2 7.0 %scatter_custom_fusion.11 = f32[4224,256]{1,0:T(8,128)} fusion(f32[4224,256]{1,0:T(8,128)} %scatter_custom_fusion.10, s32[384]{0:T(512)} %copy-done.62, f32[384,256]{1,0:T(8,128)S(1)} %convolution_divide_fusion, f32[384]{0:T(512)S(1)} %copy-done.34), kind=kCustom, calls=%fused_computation.91 | custom fusion | flops 196608 | bytes 4720128 | tf_op jit(solution)/shard_map/scatter-add | solution.py:70
  402.2 6.9 %scatter_custom_fusion.12 = f32[4224,256]{1,0:T(8,128)} fusion(f32[4224,256]{1,0:T(8,128)} %scatter_custom_fusion.11, s32[384]{0:T(512)} %copy-done.61, f32[384,256]{1,0:T(8,128)S(1)} %convolution_divide_fusion, f32[384]{0:T(512)S(1)} %copy-done.33), kind=kCustom, calls=%fused_computation.89 | custom fusion | flops 196608 | bytes 4720128 | tf_op jit(solution)/shard_map/scatter-add | solution.py:70
  409.0 6.9 %scatter_custom_fusion.13 = f32[4224,256]{1,0:T(8,128)} fusion(f32[4224,256]{1,0:T(8,128)} %scatter_custom_fusion.12, s32[384]{0:T(512)} %copy-done.60, f32[384,256]{1,0:T(8,128)S(1)} %convolution_divide_fusion, f32[384]{0:T(512)S(1)} %copy-done.32), kind=kCustom, calls=%fused_computation.87 | custom fusion | flops 196608 | bytes 4720128 | tf_op jit(solution)/shard_map/scatter-add | solution.py:70
  415.9 6.9 %scatter_custom_fusion.14 = f32[4224,256]{1,0:T(8,128)} fusion(f32[4224,256]{1,0:T(8,128)} %scatter_custom_fusion.13, s32[384]{0:T(512)} %copy-done.59, f32[384,256]{1,0:T(8,128)S(1)} %convolution_divide_fusion, f32[384]{0:T(512)S(1)} %get-tuple-element.121), kind=kCustom, calls=%fused_computation.85 | custom fusion | flops 196608 | bytes 4720128 | tf_op jit(solution)/shard_map/scatter-add | solution.py:70
  422.7 4.4 convert_reduce_fusion
  431.8 35.3 %all-reduce.11.cloned.1.call-done = (f32[2,128,256]{2,1,0:T(8,128)}, f32[2,256,256]{2,1,0:T(8,128)}, f32[2,256,172]{1,2,0:T(8,128)}) async-done(((f32[2,128,256]{2,1,0:T(8,128)}, f32[2,256,256]{2,1,0:T(8,128)}, f32[2,256,172]{1,2,0:T(8,128)}), (f32[2,128,256]{2,1,0:T(8,128)}, f32[2,256,256]{2,1,0:T(8,128)}, f32[2,256,172]{1,2,0:T(8,128)})) %all-reduce.11.cloned.1.call-update) | async-done | bytes 1138704 | tf_op jit(solution)/shard_map/psum | solution.py:180
  467.9 6.8 %all-reduce.4 = (f32[]{:T(128)}, f32[]{:T(128)}, f32[684]{0:T(1024)S(1)}) all-reduce(f32[]{:T(128)} %get-tuple-element.141, f32[]{:T(128)} %get-tuple-element.140, f32[684]{0:T(1024)S(1)} %pad_maximum_fusion.3), channel_id=1, replica_groups=mesh['hst'=4,'dev'=8] {'hst'}, use_global_device_ids=true, to_apply=%region_7.8 | all-reduce | flops 686 | bytes 5488 | tf_op jit(solution)/shard_map/psum | solution.py:180
  474.7 22.6 %all-reduce.2 = (f32[]{:T(128)}, f32[]{:T(128)}, f32[684]{0:T(1024)S(1)}) all-reduce(f32[]{:T(128)} %get-tuple-element.148, f32[]{:T(128)} %get-tuple-element.149, f32[684]{0:T(1024)S(1)} %get-tuple-element.150), channel_id=1, replica_groups=mesh['hst'=4,'dev'=8] {'dev'}, use_global_device_ids=true, to_apply=%region_8.9 | all-reduce | flops 686 | bytes 5488 | tf_op jit(solution)/shard_map/psum | solution.py:179
  500.0 52.1 %all-reduce.9.cloned.1.call-done = (f32[2,128,256]{2,1,0:T(8,128)}, f32[2,256,256]{2,1,0:T(8,128)}, f32[2,256,172]{1,2,0:T(8,128)}) async-done(((f32[2,128,256]{2,1,0:T(8,128)}, f32[2,256,256]{2,1,0:T(8,128)}, f32[2,256,172]{1,2,0:T(8,128)}), (f32[2,128,256]{2,1,0:T(8,128)}, f32[2,256,256]{2,1,0:T(8,128)}, f32[2,256,172]{1,2,0:T(8,128)})) %all-reduce.9.cloned.1.call-update) | async-done | bytes 1138704 | tf_op jit(solution)/shard_map/psum | solution.py:179
  552.1 2.8 fusion.7
  554.9 2.1 fusion.97
  557.0 3.2 fusion.3
  563.7 2.6 fusion.4
  569.1 2.6 fusion.1
  571.7 2.2 fusion.2
  576.5 1.5 fusion.104
  (261 shorter events, 60.3 us)
Async XLA Ops:
  7.2 569.3 %copy-start = (f32[2,256,256]{2,1,0:T(8,128)S(1)}, f32[2,256,256]{2,1,0:T(8,128)}, u32[]{:S(2)}) copy-start(f32[2,256,256]{2,1,0:T(8,128)} %param.60) | copy-start | bytes 1572868
  8.6 17.1 %all-to-all-start = ((s32[32,1,256]{2,1,0:T(1,128)}), s32[32,1,256]{2,1,0:T(1,128)S(1)}, u32[]{:S(2)}, u32[]{:S(2)}) async-start(s32[32,1,256]{2,1,0:T(1,128)} %all_to_all.11), calls=%async_computation | async-start | bytes 65536 | tf_op jit(solution)/shard_map/all_to_all | solution.py:12
  57.2 5.9 %copy-start.78 = (s32[64,5]{0,1:T(8,128)S(1)}, s32[64,5]{0,1:T(8,128)}, u32[]{:S(2)}) copy-start(s32[64,5]{0,1:T(8,128)} %param.37) | copy-start | bytes 3844
  57.2 6.6 %copy-start.43 = (s32[64,5]{0,1:T(8,128)S(1)}, s32[64,5]{0,1:T(8,128)}, u32[]{:S(2)}) copy-start(s32[64,5]{0,1:T(8,128)} %param.40) | copy-start | bytes 3844
  57.2 7.9 %copy-start.47 = (s32[384,10]{0,1:T(8,128)S(1)}, s32[384,10]{0,1:T(8,128)}, u32[]{:S(2)}) copy-start(s32[384,10]{0,1:T(8,128)} %param.36) | copy-start | bytes 46084
  57.2 15.0 %copy-start.19 = (s32[384,10]{0,1:T(8,128)S(1)}, s32[384,10]{0,1:T(8,128)}, u32[]{:S(2)}) copy-start(s32[384,10]{0,1:T(8,128)} %param.39) | copy-start | bytes 46084
  57.2 21.0 %copy-start.10 = (s32[4224,15]{0,1:T(8,128)S(1)}, s32[4224,15]{0,1:T(8,128)}, u32[]{:S(2)}) copy-start(s32[4224,15]{0,1:T(8,128)} %param.38) | copy-start | bytes 760324
  57.2 55.9 %all-to-all-start.1 = ((bf16[32,256,128]{2,1,0:T(8,128)(2,1)}), bf16[32,256,128]{2,1,0:T(8,128)(2,1)S(1)}, u32[]{:S(2)}, u32[]{:S(2)}) async-start(bf16[32,256,128]{2,1,0:T(8,128)(2,1)} %bitcast.106), calls=%async_computation.1 | async-start | bytes 4194304 | tf_op jit(solution)/shard_map/all_to_all | solution.py:14
  63.1 404.0 %all-reduce.11.cloned.1.call-start = ((), (), s32[]{:S(2)}) async-start(), calls=%async_computation.3 | async-start | bytes 2293760 | tf_op jit(solution)/shard_map/psum | solution.py:180
  63.1 19.0 %copy-start.44 = (f32[684]{0:T(1024)S(1)}, f32[684]{0:T(1024)}, u32[]{:S(2)}) copy-start(f32[684]{0:T(1024)} %param.46) | copy-start | bytes 8212
  63.1 19.6 %copy-start.46 = (f32[64,5]{0,1:T(8,128)S(1)}, f32[64,5]{0,1:T(8,128)}, u32[]{:S(2)}) copy-start(f32[64,5]{0,1:T(8,128)} %convert_element_type.201) | copy-start | bytes 3844
  123.7 10.5 %copy-start.25 = (s32[5120]{0:T(1024)S(1)}, s32[5120]{0:T(1024)}, u32[]{:S(2)}) copy-start(s32[5120]{0:T(1024)} %get-tuple-element.190) | copy-start | bytes 61444
  153.4 10.5 %copy-start.20 = (s32[5120]{0:T(1024)S(1)}, s32[5120]{0:T(1024)}, u32[]{:S(2)}) copy-start(s32[5120]{0:T(1024)} %get-tuple-element.193) | copy-start | bytes 61444
  163.9 9.6 %copy-start.26 = (s32[5120]{0:T(1024)S(1)}, s32[5120]{0:T(1024)}, u32[]{:S(2)}) copy-start(s32[5120]{0:T(1024)} %get-tuple-element.194) | copy-start | bytes 61444
  173.5 9.6 %copy-start.21 = (s32[5120]{0:T(1024)S(1)}, s32[5120]{0:T(1024)}, u32[]{:S(2)}) copy-start(s32[5120]{0:T(1024)} %get-tuple-element.195) | copy-start | bytes 61444
  183.0 9.6 %copy-start.27 = (s32[5120]{0:T(1024)S(1)}, s32[5120]{0:T(1024)}, u32[]{:S(2)}) copy-start(s32[5120]{0:T(1024)} %get-tuple-element.196) | copy-start | bytes 61444
  192.6 9.6 %copy-start.22 = (s32[5120]{0:T(1024)S(1)}, s32[5120]{0:T(1024)}, u32[]{:S(2)}) copy-start(s32[5120]{0:T(1024)} %get-tuple-element.197) | copy-start | bytes 61444
  202.2 9.6 %copy-start.28 = (s32[5120]{0:T(1024)S(1)}, s32[5120]{0:T(1024)}, u32[]{:S(2)}) copy-start(s32[5120]{0:T(1024)} %get-tuple-element.198) | copy-start | bytes 61444
  211.8 9.6 %copy-start.23 = (s32[5120]{0:T(1024)S(1)}, s32[5120]{0:T(1024)}, u32[]{:S(2)}) copy-start(s32[5120]{0:T(1024)} %get-tuple-element.199) | copy-start | bytes 61444
  221.4 9.6 %copy-start.29 = (s32[5120]{0:T(1024)S(1)}, s32[5120]{0:T(1024)}, u32[]{:S(2)}) copy-start(s32[5120]{0:T(1024)} %get-tuple-element.200) | copy-start | bytes 61444
  231.0 9.6 %copy-start.24 = (s32[5120]{0:T(1024)S(1)}, s32[5120]{0:T(1024)}, u32[]{:S(2)}) copy-start(s32[5120]{0:T(1024)} %get-tuple-element.201) | copy-start | bytes 61444
  240.5 9.6 %copy-start.30 = (s32[5120]{0:T(1024)S(1)}, s32[5120]{0:T(1024)}, u32[]{:S(2)}) copy-start(s32[5120]{0:T(1024)} %pad_clamp_fusion.14) | copy-start | bytes 61444
  275.6 4.0 copy-start.6
  275.6 7.6 %copy-start.56 = (s32[1024]{0:T(1024)S(1)}, s32[1024]{0:T(1024)}, u32[]{:S(2)}) copy-start(s32[1024]{0:T(1024)} %get-tuple-element.203) | copy-start | bytes 12292
  279.7 7.7 %copy-start.55 = (s32[1024]{0:T(1024)S(1)}, s32[1024]{0:T(1024)}, u32[]{:S(2)}) copy-start(s32[1024]{0:T(1024)} %get-tuple-element.204) | copy-start | bytes 12292
  283.3 8.2 %copy-start.54 = (s32[1024]{0:T(1024)S(1)}, s32[1024]{0:T(1024)}, u32[]{:S(2)}) copy-start(s32[1024]{0:T(1024)} %get-tuple-element.205) | copy-start | bytes 12292
  287.3 8.3 %copy-start.53 = (s32[1024]{0:T(1024)S(1)}, s32[1024]{0:T(1024)}, u32[]{:S(2)}) copy-start(s32[1024]{0:T(1024)} %get-tuple-element.206) | copy-start | bytes 12292
  291.4 8.3 %copy-start.52 = (s32[1024]{0:T(1024)S(1)}, s32[1024]{0:T(1024)}, u32[]{:S(2)}) copy-start(s32[1024]{0:T(1024)} %get-tuple-element.207) | copy-start | bytes 12292
  295.7 8.2 %copy-start.51 = (s32[1024]{0:T(1024)S(1)}, s32[1024]{0:T(1024)}, u32[]{:S(2)}) copy-start(s32[1024]{0:T(1024)} %get-tuple-element.208) | copy-start | bytes 12292
  299.7 8.1 %copy-start.50 = (s32[1024]{0:T(1024)S(1)}, s32[1024]{0:T(1024)}, u32[]{:S(2)}) copy-start(s32[1024]{0:T(1024)} %get-tuple-element.209) | copy-start | bytes 12292
  303.8 8.2 %copy-start.49 = (s32[1024]{0:T(1024)S(1)}, s32[1024]{0:T(1024)}, u32[]{:S(2)}) copy-start(s32[1024]{0:T(1024)} %get-tuple-element.210) | copy-start | bytes 12292
  307.9 8.2 %copy-start.48 = (s32[1024]{0:T(1024)S(1)}, s32[1024]{0:T(1024)}, u32[]{:S(2)}) copy-start(s32[1024]{0:T(1024)} %get-tuple-element.211) | copy-start | bytes 12292
  311.9 9.3 %copy-start.32 = (f32[384]{0:T(512)S(1)}, f32[384]{0:T(512)}, u32[]{:S(2)}) copy-start(f32[384]{0:T(512)} %get-tuple-element.122) | copy-start | bytes 4612
  311.9 9.4 %copy-start.33 = (f32[384]{0:T(512)S(1)}, f32[384]{0:T(512)}, u32[]{:S(2)}) copy-start(f32[384]{0:T(512)} %get-tuple-element.123) | copy-start | bytes 4612
  311.9 9.4 %copy-start.34 = (f32[384]{0:T(512)S(1)}, f32[384]{0:T(512)}, u32[]{:S(2)}) copy-start(f32[384]{0:T(512)} %get-tuple-element.124) | copy-start | bytes 4612
  311.9 9.4 %copy-start.35 = (f32[384]{0:T(512)S(1)}, f32[384]{0:T(512)}, u32[]{:S(2)}) copy-start(f32[384]{0:T(512)} %get-tuple-element.125) | copy-start | bytes 4612
  311.9 9.4 %copy-start.36 = (f32[384]{0:T(512)S(1)}, f32[384]{0:T(512)}, u32[]{:S(2)}) copy-start(f32[384]{0:T(512)} %get-tuple-element.126) | copy-start | bytes 4612
  312.0 9.4 %copy-start.37 = (f32[384]{0:T(512)S(1)}, f32[384]{0:T(512)}, u32[]{:S(2)}) copy-start(f32[384]{0:T(512)} %get-tuple-element.127) | copy-start | bytes 4612
  312.0 9.4 %copy-start.38 = (f32[384]{0:T(512)S(1)}, f32[384]{0:T(512)}, u32[]{:S(2)}) copy-start(f32[384]{0:T(512)} %get-tuple-element.128) | copy-start | bytes 4612
  312.0 9.4 %copy-start.39 = (f32[384]{0:T(512)S(1)}, f32[384]{0:T(512)}, u32[]{:S(2)}) copy-start(f32[384]{0:T(512)} %get-tuple-element.129) | copy-start | bytes 4612
  312.0 9.4 %copy-start.41 = (f32[384]{0:T(512)S(1)}, f32[384]{0:T(512)}, u32[]{:S(2)}) copy-start(f32[384]{0:T(512)} %get-tuple-element.120) | copy-start | bytes 4612
  312.0 9.4 %copy-start.58 = (f32[384]{0:T(512)S(1)}, f32[384]{0:T(512)}, u32[]{:S(2)}) copy-start(f32[384]{0:T(512)} %broadcast_maximum_fusion.1) | copy-start | bytes 4612
  316.1 7.4 %copy-start.79 = (f32[256]{0:T(256)S(1)}, f32[256]{0:T(256)}, u32[]{:S(2)}) copy-start(f32[256]{0:T(256)} %get-tuple-element.174) | copy-start | bytes 3076
  323.5 9.0 %copy-start.14 = (bf16[384,256]{1,0:T(8,128)(2,1)}, bf16[384,256]{1,0:T(8,128)(2,1)S(1)}, u32[]{:S(2)}) copy-start(bf16[384,256]{1,0:T(8,128)(2,1)S(1)} %divide_convert_fusion.1) | copy-start | bytes 589828
  353.6 7.3 %copy-start.40 = (f32[384]{0:T(512)S(1)}, f32[384]{0:T(512)}, u32[]{:S(2)}) copy-start(f32[384]{0:T(512)} %get-tuple-element.129) | copy-start | bytes 4612
  429.3 38.6 %copy-start.69 = (f32[172]{0:T(256)S(1)}, f32[172]{0:T(256)}, u32[]{:S(2)}) copy-start(f32[172]{0:T(256)} %get-tuple-element.161) | copy-start | bytes 2068
  429.3 38.6 %copy-start.70 = (f32[256]{0:T(256)S(1)}, f32[256]{0:T(256)}, u32[]{:S(2)}) copy-start(f32[256]{0:T(256)} %get-tuple-element.159) | copy-start | bytes 3076
  429.3 69.4 %copy-start.45 = (f32[684]{0:T(1024)S(1)}, f32[684]{0:T(1024)}, u32[]{:S(2)}) copy-start(f32[684]{0:T(1024)} %param.46) | copy-start | bytes 8212
  429.3 69.4 %copy-start.71 = (f32[684]{0:T(1024)S(1)}, f32[684]{0:T(1024)}, u32[]{:S(2)}) copy-start(f32[684]{0:T(1024)} %param.48) | copy-start | bytes 8212
  429.3 69.4 %copy-start.72 = (f32[684]{0:T(1024)S(1)}, f32[684]{0:T(1024)}, u32[]{:S(2)}) copy-start(f32[684]{0:T(1024)} %param.47) | copy-start | bytes 8212
  430.1 122.0 %copy-start.88 = (f32[2,128,128]{2,1,0:T(8,128)S(1)}, f32[2,128,128]{2,1,0:T(8,128)}, u32[]{:S(2)}) copy-start(f32[2,128,128]{2,1,0:T(8,128)} %param.50) | copy-start | bytes 393220
  431.0 124.0 %copy-start.89 = (f32[2,128,128]{2,1,0:T(8,128)S(1)}, f32[2,128,128]{2,1,0:T(8,128)}, u32[]{:S(2)}) copy-start(f32[2,128,128]{2,1,0:T(8,128)} %param.56) | copy-start | bytes 393220
  431.7 125.3 %copy-start.16 = (f32[2,256,256]{2,1,0:T(8,128)S(1)}, f32[2,256,256]{2,1,0:T(8,128)}, u32[]{:S(2)}) copy-start(f32[2,256,256]{2,1,0:T(8,128)} %param.53) | copy-start | bytes 1572868
  431.7 120.4 %all-reduce.9.cloned.1.call-start = ((), (), s32[]{:S(2)}) async-start(), calls=%async_computation.2 | async-start | bytes 2293760 | tf_op jit(solution)/shard_map/psum | solution.py:179
  467.1 93.1 %copy-start.87 = (f32[2,172,172]{2,0,1:T(2,128)S(1)}, f32[2,172,172]{2,0,1:T(2,128)}, u32[]{:S(2)}) copy-start(f32[2,172,172]{2,0,1:T(2,128)} %param.55) | copy-start | bytes 710020
  552.1 8.1 %copy-start.86 = (f32[2,256,172]{1,2,0:T(8,128)S(1)}, f32[2,256,172]{1,2,0:T(8,128)}, u32[]{:S(2)}) copy-start(f32[2,256,172]{1,2,0:T(8,128)} %get-tuple-element.147) | copy-start | bytes 1056772
  554.9 7.5 %copy-start.80 = (f32[2,256,256]{2,1,0:T(8,128)S(1)}, f32[2,256,256]{2,1,0:T(8,128)}, u32[]{:S(2)}) copy-start(f32[2,256,256]{2,1,0:T(8,128)} %param.58) | copy-start | bytes 1572868
  557.0 6.7 %copy-start.81 = (f32[2,256,256]{2,1,0:T(8,128)S(1)}, f32[2,256,256]{2,1,0:T(8,128)}, u32[]{:S(2)}) copy-start(f32[2,256,256]{2,1,0:T(8,128)} %param.52) | copy-start | bytes 1572868
  561.3 5.0 copy-start.9
  561.4 5.0 copy-start.18
  563.7 5.3 copy-start.82
  563.7 5.3 copy-start.85
  566.4 5.3 copy-start.83
  569.1 4.8 copy-start.84
  (30 other events, 64.9 us)
Sparse Core Ops, SparseCore 0:
  431.8 35.2 all-reduce.10
  470.9 81.1 all-reduce.8
